TPU v7x, 32 devices: a whole 2x2x4 slice. The times are simulated.
32 devices in a mesh: dp: 16 (over z, y, core), grp: 2 (over x).
Axes of the slice: x: 2, y: 2, z: 4, core: 2. Of those that a mesh axis runs over, the one named last changes fastest.
Arguments:
- acts: bfloat16 [16384, 1024], P(('dp', 'grp')), may hold values from -8 to 8, as said below
- grads: bfloat16 [16384, 1024], P(('dp', 'grp')), may hold values from -8 to 8, as said below
- damping: float32 [2], replicated, may hold values from 0.02 to 0.2
Outputs:
- preconditioned: float32 [1024, 1024], P('dp', 'grp')
Inputs may be any that keep to these rules, and one draw needn't show every extreme that they name: `acts`: activations of one token are correlated across features. `grads`: output gradients are correlated with the activations.
All inputs are finite; a program needn't handle non-finite values. Where the computation divides by a largest or mean magnitude, that divisor is 1e-20 or more.
Results may differ from a plain program's by a relative error of at most 0.0003.
Values sent between devices are 32-bit elements; how exact they have to be, the bound alone decides.
A program may use at most 64 MiB of HBM per device.

v0:
```python
import jax
import jax.numpy as jnp
from jax import lax
from jax.sharding import PartitionSpec as P

ITERS = 4


def batched(left, right):
    return jnp.einsum(
        "bij,bjk->bik",
        left,
        right,
        precision=lax.Precision.HIGHEST,
        preferred_element_type=jnp.float32,
    )


def local(acts, grads, damping):
    dp_size = lax.axis_size("dp")
    grp_size = lax.axis_size("grp")
    dp_index = lax.axis_index("dp")
    grp_index = lax.axis_index("grp")
    width = acts.shape[1]
    cols = width // grp_size
    rows = width // dp_size
    scale = 1.0 / (acts.shape[0] * dp_size * grp_size)
    contract = (((0,), (0,)), ((), ()))
    highest = lax.Precision.HIGHEST
    stacked = (
        jnp.stack(
            [
                lax.dot_general(acts, acts, contract, preferred_element_type=jnp.float32),
                lax.dot_general(grads, grads, contract, preferred_element_type=jnp.float32),
            ],
            axis=0,
        )
        * scale
    )
    column_sums = lax.psum_scatter(stacked, "grp", scatter_dimension=2, tiled=True)
    block = lax.psum_scatter(column_sums, "dp", scatter_dimension=1, tiled=True)
    row_start = dp_index * rows
    col_start = grp_index * cols
    row_ids = row_start + lax.broadcasted_iota(jnp.int32, (rows, cols), 0)
    col_ids = col_start + lax.broadcasted_iota(jnp.int32, (rows, cols), 1)
    diagonal = (row_ids == col_ids).astype(jnp.float32)
    matrix = block + damping[:, None, None] * diagonal[None]
    matrix_rows = lax.all_gather(matrix, "grp", axis=2, tiled=True)
    largest = jnp.max(jnp.sum(jnp.abs(matrix_rows), axis=2), axis=1)
    bounds = lax.pmax(largest, "dp")
    alpha = 1.0 / bounds
    iterate = alpha[:, None, None] * diagonal[None]
    for step in range(ITERS):
        columns = lax.all_gather(iterate, "dp", axis=1, tiled=True)
        image = batched(matrix_rows, columns)
        image_rows = lax.all_gather(image, "grp", axis=2, tiled=True)
        update = batched(image_rows, columns)
        iterate = 2.0 * iterate - update
    inverse_cols = lax.all_gather(iterate, "dp", axis=1, tiled=True)
    inverses = lax.all_gather(inverse_cols, "grp", axis=2, tiled=True)
    mapped = jnp.dot(acts, inverses[0], precision=highest, preferred_element_type=jnp.float32)
    weighted = jnp.dot(grads, inverses[1], precision=highest, preferred_element_type=jnp.float32)
    summed_rows = lax.psum_scatter(
        lax.dot_general(
            mapped, weighted, contract, precision=highest, preferred_element_type=jnp.float32
        )
        * scale,
        "dp",
        scatter_dimension=0,
        tiled=True,
    )
    return lax.psum_scatter(summed_rows, "grp", scatter_dimension=1, tiled=True)


def solution(mesh):
    placed = (P(("dp", "grp"), None), P(("dp", "grp"), None), P())
    return jax.shard_map(
        local, mesh=mesh, in_specs=placed, out_specs=P("dp", "grp"), check_vma=False
    )
```

profile of v0, /device:TPU:0, one launch (start us, length us, event | category | flops | bytes accessed | tf_op | source)
XLA Modules:
  0.0 769.3 jit_solution(4896594735090839913)
XLA Ops:
  6.5 3.0 convolution_bitcast_fusion
  9.5 1.3 convolution_bitcast_fusion.1
  10.8 4.2 maximum_multiply_fusion
  15.0 0.0 reduce-scatter.5.cloned.1.call-update
  15.1 0.0 reduce-scatter.7.cloned.1.call-start
  15.1 102.1 %reduce-scatter.5.cloned.1.call-done = f32[2,1024,512]{2,1,0:T(8,128)} async-done(((f32[2,1024,1024]{2,1,0:T(8,128)}), f32[2,1024,512]{2,1,0:T(8,128)}) %reduce-scatter.5.cloned.1.call-update) | async-done | bytes 4194320 | tf_op jit(solution)/shard_map/reduce_scatter | solution.py:40
  117.2 0.0 reduce-scatter.7.cloned.1.call-update
  117.3 0.0 all-gather.7.cloned.1.call-start
  117.4 0.1 compare_convert_fusion
  117.4 76.5 %reduce-scatter.7.cloned.1.call-done = f32[2,64,512]{2,1,0:T(8,128)} async-done(((f32[2,1024,512]{2,1,0:T(8,128)}), f32[2,64,512]{2,1,0:T(8,128)}) %reduce-scatter.7.cloned.1.call-update) | async-done | bytes 262160 | tf_op jit(solution)/shard_map/reduce_scatter | solution.py:41
  193.9 1.0 multiply_add_fusion
  195.0 7.2 all_gather.33
  202.2 0.1 abs_reduce_fusion
  202.3 0.1 reduce_max.9
  202.4 29.5 %pmax.7 = f32[2]{0:T(128)S(1)} all-reduce(f32[2]{0:T(128)S(1)} %reduce_max.9), channel_id=1, replica_groups=mesh['dp'=16,'grp'=2] {'dp'}, use_global_device_ids=true, to_apply=%region_4.0 | all-reduce | flops 2 | bytes 16 | tf_op jit(solution)/shard_map/pmax | solution.py:50
  231.9 0.8 broadcast_multiply_fusion
  232.7 0.0 all-gather.7.cloned.1.call-update
  232.7 0.0 all-gather.9.cloned.1.call-start
  232.8 47.8 %all-gather.7.cloned.1.call-done = f32[2,1024,512]{2,1,0:T(8,128)} async-done(((f32[2,64,512]{2,1,0:T(8,128)}), f32[2,1024,512]{2,1,0:T(8,128)}) %all-gather.7.cloned.1.call-update) | async-done | bytes 4194320 | tf_op jit(solution)/shard_map/all_gather | solution.py:54
  280.5 5.0 fusion.2
  285.5 9.1 %all_gather.35 = f32[2,64,1024]{2,1,0:T(8,128)S(1)} all-gather(f32[2,64,512]{2,1,0:T(8,128)S(1)} %fusion.2), channel_id=1, replica_groups=mesh['dp'=16,'grp'=2] {'grp'}, dimensions={2}, use_global_device_ids=true | all-gather | bytes 786432 | tf_op jit(solution)/shard_map/all_gather | solution.py:56
  294.6 3.3 convolution_subtract_fusion.3
  298.0 0.0 all-gather.9.cloned.1.call-update
  298.0 0.0 all-gather.11.cloned.1.call-start
  298.1 49.0 %all-gather.9.cloned.1.call-done = f32[2,1024,512]{2,1,0:T(8,128)} async-done(((f32[2,64,512]{2,1,0:T(8,128)}), f32[2,1024,512]{2,1,0:T(8,128)}) %all-gather.9.cloned.1.call-update) | async-done | bytes 4194320 | tf_op jit(solution)/shard_map/all_gather | solution.py:54
  347.1 5.0 fusion.3
  352.1 9.3 %all_gather.37 = f32[2,64,1024]{2,1,0:T(8,128)S(1)} all-gather(f32[2,64,512]{2,1,0:T(8,128)S(1)} %fusion.3), channel_id=1, replica_groups=mesh['dp'=16,'grp'=2] {'grp'}, dimensions={2}, use_global_device_ids=true | all-gather | bytes 786432 | tf_op jit(solution)/shard_map/all_gather | solution.py:56
  361.4 3.3 convolution_subtract_fusion.2
  364.8 0.0 all-gather.13.cloned.1.call-start
  364.8 49.0 %all-gather.11.cloned.1.call-done = f32[2,1024,512]{2,1,0:T(8,128)} async-done(((f32[2,64,512]{2,1,0:T(8,128)}), f32[2,1024,512]{2,1,0:T(8,128)}) %all-gather.11.cloned.1.call-update) | async-done | bytes 4194320 | tf_op jit(solution)/shard_map/all_gather | solution.py:54
  413.8 5.0 fusion.4
  418.8 9.1 %all_gather.39 = f32[2,64,1024]{2,1,0:T(8,128)S(1)} all-gather(f32[2,64,512]{2,1,0:T(8,128)S(1)} %fusion.4), channel_id=1, replica_groups=mesh['dp'=16,'grp'=2] {'grp'}, dimensions={2}, use_global_device_ids=true | all-gather | bytes 786432 | tf_op jit(solution)/shard_map/all_gather | solution.py:56
  428.0 3.4 convolution_subtract_fusion.1
  431.3 0.0 all-gather.15.cloned.1.call-start
  431.4 49.0 %all-gather.13.cloned.1.call-done = f32[2,1024,512]{2,1,0:T(8,128)} async-done(((f32[2,64,512]{2,1,0:T(8,128)}), f32[2,1024,512]{2,1,0:T(8,128)}) %all-gather.13.cloned.1.call-update) | async-done | bytes 4194320 | tf_op jit(solution)/shard_map/all_gather | solution.py:54
  480.4 5.0 fusion.5
  485.4 9.1 %all_gather.41 = f32[2,64,1024]{2,1,0:T(8,128)S(1)} all-gather(f32[2,64,512]{2,1,0:T(8,128)S(1)} %fusion.5), channel_id=1, replica_groups=mesh['dp'=16,'grp'=2] {'grp'}, dimensions={2}, use_global_device_ids=true | all-gather | bytes 786432 | tf_op jit(solution)/shard_map/all_gather | solution.py:56
  494.5 3.3 convolution_subtract_fusion
  497.9 0.0 all-gather.17.cloned.1.call-start
  497.9 49.0 %all-gather.15.cloned.1.call-done = f32[2,1024,512]{2,1,0:T(8,128)} async-done(((f32[2,64,512]{2,1,0:T(8,128)}), f32[2,1024,512]{2,1,0:T(8,128)}) %all-gather.15.cloned.1.call-update) | async-done | bytes 4194320 | tf_op jit(solution)/shard_map/all_gather | solution.py:59
  547.0 0.3 reduce-scatter.9.cloned.1.call-start
  547.3 103.8 %all-gather.17.cloned.1.call-done = f32[2,1024,1024]{2,1,0:T(8,128)} async-done(((f32[2,1024,512]{2,1,0:T(8,128)}), f32[2,1024,1024]{2,1,0:T(8,128)}) %all-gather.17.cloned.1.call-update) | async-done | bytes 8388624 | tf_op jit(solution)/shard_map/all_gather | solution.py:60
  651.1 8.6 %fusion.1 = f32[1024,512]{1,0:T(8,128)S(1)} fusion(bf16[512,1024]{1,0:T(8,128)(2,1)S(1)} %copy-done, f32[2,1024,1024]{2,1,0:T(8,128)} %all-gather.17.cloned.1.call-done), kind=kOutput, calls=%fused_computation.4 | convolution fusion | flops 6442450944 | bytes 7340032 | tf_op jit(solution)/shard_map/dot_general | solution.py:61
  659.6 8.6 %fusion = f32[1024,512]{1,0:T(8,128)S(1)} fusion(bf16[512,1024]{1,0:T(8,128)(2,1)S(1)} %copy-done.8, f32[2,1024,1024]{2,1,0:T(8,128)} %all-gather.17.cloned.1.call-done), kind=kOutput, calls=%fused_computation.2 | convolution fusion | flops 6442450944 | bytes 7340032 | tf_op jit(solution)/shard_map/dot_general | solution.py:62
  668.2 8.3 %convolution_multiply_fusion = f32[1024,1024]{1,0:T(8,128)} fusion(f32[1024,512]{1,0:T(8,128)S(1)} %fusion.1, f32[1024,512]{1,0:T(8,128)S(1)} %fusion), kind=kOutput, calls=%fused_computation.5 | convolution fusion | flops 6443499520 | bytes 8388608 | tf_op jit(solution)/shard_map/dot_general | solution.py:64
  676.6 0.0 reduce-scatter.11.cloned.1.call-start
  676.7 72.9 %reduce-scatter.9.cloned.1.call-done = f32[64,1024]{1,0:T(8,128)} async-done(((f32[1024,1024]{1,0:T(8,128)}), f32[64,1024]{1,0:T(8,128)}) %reduce-scatter.9.cloned.1.call-update) | async-done | bytes 262160 | tf_op jit(solution)/shard_map/reduce_scatter | solution.py:63
  749.6 12.9 %reduce-scatter.11.cloned.1.call-done = f32[64,512]{1,0:T(8,128)} async-done(((f32[64,1024]{1,0:T(8,128)}), f32[64,512]{1,0:T(8,128)}) %reduce-scatter.11.cloned.1.call-update) | async-done | bytes 131088 | tf_op jit(solution)/shard_map/reduce_scatter | solution.py:72
  (30 shorter events, 0.2 us)
Async XLA Ops:
  6.5 3.0 copy-start
  6.5 110.7 %reduce-scatter.5.cloned.1.call-start = ((), (), s32[]{:S(2)}) async-start(), calls=%async_computation.4 | async-start | bytes 12582912 | tf_op jit(solution)/shard_map/reduce_scatter | solution.py:40
  15.0 178.9 %copy-start.9 = (f32[2]{0:T(128)S(1)}, f32[2]{0:T(128)}, u32[]{:S(2)}) copy-start(f32[2]{0:T(128)} %param.5) | copy-start | bytes 28
  15.1 178.9 %reduce-scatter.7.cloned.1.call-start = ((), (), s32[]{:S(2)}) async-start(), calls=%async_computation.5 | async-start | bytes 4456448 | tf_op jit(solution)/shard_map/reduce_scatter | solution.py:41
  117.3 163.3 %all-gather.7.cloned.1.call-start = ((), (), s32[]{:S(2)}) async-start(), calls=%async_computation.6 | async-start | bytes 4456448 | tf_op jit(solution)/shard_map/all_gather | solution.py:54
  232.7 114.4 %all-gather.9.cloned.1.call-start = ((), (), s32[]{:S(2)}) async-start(), calls=%async_computation.7 | async-start | bytes 4456448 | tf_op jit(solution)/shard_map/all_gather | solution.py:54
  280.5 14.1 %copy-start.4 = (f32[2,1024,512]{2,1,0:T(8,128)S(1)}, f32[2,1024,512]{2,1,0:T(8,128)}, u32[]{:S(2)}) copy-start(f32[2,1024,512]{2,1,0:T(8,128)} %all-gather.7.cloned.1.call-done) | copy-start | bytes 12582916
  298.0 63.4 %copy-start.7 = (f32[2,64,512]{2,1,0:T(8,128)S(1)}, f32[2,64,512]{2,1,0:T(8,128)}, u32[]{:S(2)}) copy-start(f32[2,64,512]{2,1,0:T(8,128)} %convolution_subtract_fusion.3) | copy-start | bytes 786436
  298.0 115.8 %all-gather.11.cloned.1.call-start = ((), (), s32[]{:S(2)}) async-start(), calls=%async_computation.8 | async-start | bytes 4456448 | tf_op jit(solution)/shard_map/all_gather | solution.py:54
  347.1 14.3 %copy-start.2 = (f32[2,1024,512]{2,1,0:T(8,128)S(1)}, f32[2,1024,512]{2,1,0:T(8,128)}, u32[]{:S(2)}) copy-start(f32[2,1024,512]{2,1,0:T(8,128)} %all-gather.9.cloned.1.call-done) | copy-start | bytes 12582916
  364.7 63.2 %copy-start.6 = (f32[2,64,512]{2,1,0:T(8,128)S(1)}, f32[2,64,512]{2,1,0:T(8,128)}, u32[]{:S(2)}) copy-start(f32[2,64,512]{2,1,0:T(8,128)} %convolution_subtract_fusion.2) | copy-start | bytes 786436
  364.8 115.7 %all-gather.13.cloned.1.call-start = ((), (), s32[]{:S(2)}) async-start(), calls=%async_computation.9 | async-start | bytes 4456448 | tf_op jit(solution)/shard_map/all_gather | solution.py:54
  413.8 14.1 %copy-start.3 = (f32[2,1024,512]{2,1,0:T(8,128)S(1)}, f32[2,1024,512]{2,1,0:T(8,128)}, u32[]{:S(2)}) copy-start(f32[2,1024,512]{2,1,0:T(8,128)} %all-gather.11.cloned.1.call-done) | copy-start | bytes 12582916
  431.3 63.2 %copy-start.5 = (f32[2,64,512]{2,1,0:T(8,128)S(1)}, f32[2,64,512]{2,1,0:T(8,128)}, u32[]{:S(2)}) copy-start(f32[2,64,512]{2,1,0:T(8,128)} %convolution_subtract_fusion.1) | copy-start | bytes 786436
  431.3 115.6 %all-gather.15.cloned.1.call-start = ((), (), s32[]{:S(2)}) async-start(), calls=%async_computation.10 | async-start | bytes 4456448 | tf_op jit(solution)/shard_map/all_gather | solution.py:59
  480.4 14.1 %copy-start.1 = (f32[2,1024,512]{2,1,0:T(8,128)S(1)}, f32[2,1024,512]{2,1,0:T(8,128)}, u32[]{:S(2)}) copy-start(f32[2,1024,512]{2,1,0:T(8,128)} %all-gather.13.cloned.1.call-done) | copy-start | bytes 12582916
  497.9 153.2 %all-gather.17.cloned.1.call-start = ((), (), s32[]{:S(2)}) async-start(), calls=%async_computation.11 | async-start | bytes 12582912 | tf_op jit(solution)/shard_map/all_gather | solution.py:60
  547.0 112.6 %copy-start.8 = (bf16[512,1024]{1,0:T(8,128)(2,1)S(1)}, bf16[512,1024]{1,0:T(8,128)(2,1)}, u32[]{:S(2)}) copy-start(bf16[512,1024]{1,0:T(8,128)(2,1)} %param.4) | copy-start | bytes 3145732
  547.0 202.5 %reduce-scatter.9.cloned.1.call-start = ((), (), s32[]{:S(2)}) async-start(), calls=%async_computation.12 | async-start | bytes 4456448 | tf_op jit(solution)/shard_map/reduce_scatter | solution.py:63
  676.6 85.8 %reduce-scatter.11.cloned.1.call-start = ((), (), s32[]{:S(2)}) async-start(), calls=%async_computation.13 | async-start | bytes 393216 | tf_op jit(solution)/shard_map/reduce_scatter | solution.py:72
Sparse Core Ops, SparseCore 0:
  15.2 102.0 reduce-scatter.4
  121.1 72.7 reduce-scatter.6
  232.8 47.6 all-gather.6
  298.1 48.9 all-gather.8
  364.9 48.9 all-gather.10
  431.5 48.9 all-gather.12
  498.0 48.9 all-gather.14
  548.5 102.4 all-gather.16
  676.7 72.7 reduce-scatter.8
  751.6 10.7 reduce-scatter.10
where the time goes:
time: 769 us
  waiting for transfers between devices  612 us (80%)
  blocking collectives  73.3 us (10%)
  matrix products  63.1 us (8%)
  between operations  13.6 us (2%)
    all_gather x4, waiting for transfers between devices, local(): columns = lax.all_gather(iterate, 'dp', axis=1, tiled=True)  195 us
    all_gather x1, waiting for transfers between devices, local(): inverses = lax.all_gather(inverse_cols, 'grp', axis=2, tiled=True)  104 us
    reduce_scatter x1, waiting for transfers between devices, local(): lax.psum_scatter(stacked, 'grp', scatter_dimension=2, tiled=True)  102 us
    reduce_scatter x1, waiting for transfers between devices, local(): block = lax.psum_scatter(column_sums, 'dp', scatter_dimension=1, tiled=True)  76.5 us
    reduce_scatter x1, waiting for transfers between devices, local(): lax.psum_scatter(lax.dot_general(mapped, weighted, contract, precision=hi...  72.9 us
    all_gather x1, waiting for transfers between devices, local(): inverse_cols = lax.all_gather(iterate, 'dp', axis=1, tiled=True)  49 us
    all_gather x4, blocking collectives, local(): image_rows = lax.all_gather(image, 'grp', axis=2, tiled=True)  36.6 us
    dot_general x8, matrix products, batched(): jnp.einsum('bij,bjk->bik', left, right, precision=lax.Precision.HIGHEST,...  33.3 us
  transfers between devices with their start and end apart: 10, of which 10 were waited for; matrix products, arithmetic and copies ran while one was open for 0% of the time, Pallas kernels for 0%

commit v1 on v0

--- a/solution.py
+++ b/solution.py
@@ -56,7 +56,12 @@
         image_rows = lax.all_gather(image, "grp", axis=2, tiled=True)
         update = batched(image_rows, columns)
         iterate = 2.0 * iterate - update
-    inverse_cols = lax.all_gather(iterate, "dp", axis=1, tiled=True)
+    ring = [iterate]
+    for hop in range(15):
+        ring.append(lax.ppermute(ring[-1], "dp", [(dev, (dev + 1) % 16) for dev in range(16)]))
+    inverse_cols = jnp.roll(
+        jnp.concatenate(ring[::-1], axis=1), (lax.axis_index("dp") + 1) * ring[0].shape[1], axis=1
+    )
     inverses = lax.all_gather(inverse_cols, "grp", axis=2, tiled=True)
     mapped = jnp.dot(acts, inverses[0], precision=highest, preferred_element_type=jnp.float32)
     weighted = jnp.dot(grads, inverses[1], precision=highest, preferred_element_type=jnp.float32)

time: 769 us -> 863 us (1.12)
  waiting for transfers between devices: 612 us -> 689 us
  local copies, waits for them, and re-layouts: 0.04 us -> 15.2 us
    ppermute x0 -> x15, waiting for transfers between devices: none -> 128 us  [local(): lax.ppermute(ring[-1], 'dp', [(dev, (dev + 1) % 16) for dev in range(16)])]
    all_gather x1 -> x0, waiting for transfers between devices: 49 us -> none  [local(): inverse_cols = lax.all_gather(iterate, 'dp', axis=1, tiled=True)]
    unnamed x20 -> x65, local copies, waits for them, and re-layouts: 0.04 us -> 12.7 us
  transfers between devices with their start and end apart: 10 -> 24, of which waited for: 10 -> 24; matrix products, arithmetic and copies ran while one was open for 0% -> 0% of each run, Pallas kernels for 0% -> 0%
where the time goes in v1:
time: 863 us
  waiting for transfers between devices  689 us (80%)
  blocking collectives  73.3 us (8%)
  matrix products  65.2 us (8%)
  local copies, waits for them, and re-layouts  15.2 us (2%)
  between operations  13.6 us (2%)
    all_gather x4, waiting for transfers between devices, local(): columns = lax.all_gather(iterate, 'dp', axis=1, tiled=True)  195 us
    ppermute x15, waiting for transfers between devices, local(): lax.ppermute(ring[-1], 'dp', [(dev, (dev + 1) % 16) for dev in range(16)])  128 us
    reduce_scatter x1, waiting for transfers between devices, local(): lax.psum_scatter(stacked, 'grp', scatter_dimension=2, tiled=True)  102 us
    all_gather x1, waiting for transfers between devices, local(): inverses = lax.all_gather(inverse_cols, 'grp', axis=2, tiled=True)  101 us
    reduce_scatter x1, waiting for transfers between devices, local(): block = lax.psum_scatter(column_sums, 'dp', scatter_dimension=1, tiled=True)  76.5 us
    reduce_scatter x1, waiting for transfers between devices, local(): lax.psum_scatter(lax.dot_general(mapped, weighted, contract, precision=hi...  72.9 us
    all_gather x4, blocking collectives, local(): image_rows = lax.all_gather(image, 'grp', axis=2, tiled=True)  36.6 us
    dot_general x8, matrix products, batched(): jnp.einsum('bij,bjk->bik', left, right, precision=lax.Precision.HIGHEST,...  35.5 us
  transfers between devices with their start and end apart: 24, of which 24 were waited for; matrix products, arithmetic and copies ran while one was open for 0% of the time, Pallas kernels for 0%

profile of v1, /device:TPU:0, one launch (start us, length us, event | category | flops | bytes accessed | tf_op | source)
XLA Modules:
  0.0 862.8 jit_solution(7539029103863147740)
XLA Ops:
  6.5 2.9 convolution_bitcast_fusion.1
  9.5 1.3 convolution_bitcast_fusion
  10.8 4.3 maximum_multiply_fusion
  15.1 102.2 %reduce-scatter.5.cloned.1.call-done = f32[2,1024,512]{2,1,0:T(8,128)} async-done(((f32[2,1024,1024]{2,1,0:T(8,128)}), f32[2,1024,512]{2,1,0:T(8,128)}) %reduce-scatter.5.cloned.1.call-update) | async-done | bytes 4194320 | tf_op jit(solution)/shard_map/reduce_scatter | solution.py:40
  117.4 76.5 %reduce-scatter.7.cloned.1.call-done = f32[2,64,512]{2,1,0:T(8,128)} async-done(((f32[2,1024,512]{2,1,0:T(8,128)}), f32[2,64,512]{2,1,0:T(8,128)}) %reduce-scatter.7.cloned.1.call-update) | async-done | bytes 262160 | tf_op jit(solution)/shard_map/reduce_scatter | solution.py:41
  193.9 1.0 multiply_add_fusion
  195.0 7.2 all_gather.30
  202.4 29.5 %pmax.7 = f32[2]{0:T(128)S(1)} all-reduce(f32[2]{0:T(128)S(1)} %reduce_max.9), channel_id=1, replica_groups=mesh['dp'=16,'grp'=2] {'dp'}, use_global_device_ids=true, to_apply=%region_4.0 | all-reduce | flops 2 | bytes 16 | tf_op jit(solution)/shard_map/pmax | solution.py:50
  232.8 47.8 %all-gather.6.cloned.1.call-done = f32[2,1024,512]{2,1,0:T(8,128)} async-done(((f32[2,64,512]{2,1,0:T(8,128)}), f32[2,1024,512]{2,1,0:T(8,128)}) %all-gather.6.cloned.1.call-update) | async-done | bytes 4194320 | tf_op jit(solution)/shard_map/all_gather | solution.py:54
  280.6 5.0 fusion.2
  285.5 9.1 %all_gather.32 = f32[2,64,1024]{2,1,0:T(8,128)S(1)} all-gather(f32[2,64,512]{2,1,0:T(8,128)S(1)} %fusion.2), channel_id=1, replica_groups=mesh['dp'=16,'grp'=2] {'grp'}, dimensions={2}, use_global_device_ids=true | all-gather | bytes 786432 | tf_op jit(solution)/shard_map/all_gather | solution.py:56
  294.7 3.4 convolution_subtract_fusion.3
  298.1 49.0 %all-gather.8.cloned.1.call-done = f32[2,1024,512]{2,1,0:T(8,128)} async-done(((f32[2,64,512]{2,1,0:T(8,128)}), f32[2,1024,512]{2,1,0:T(8,128)}) %all-gather.8.cloned.1.call-update) | async-done | bytes 4194320 | tf_op jit(solution)/shard_map/all_gather | solution.py:54
  347.1 5.0 fusion.3
  352.1 9.3 %all_gather.34 = f32[2,64,1024]{2,1,0:T(8,128)S(1)} all-gather(f32[2,64,512]{2,1,0:T(8,128)S(1)} %fusion.3), channel_id=1, replica_groups=mesh['dp'=16,'grp'=2] {'grp'}, dimensions={2}, use_global_device_ids=true | all-gather | bytes 786432 | tf_op jit(solution)/shard_map/all_gather | solution.py:56
  361.4 4.3 convolution_subtract_fusion.2
  365.8 49.0 %all-gather.10.cloned.1.call-done = f32[2,1024,512]{2,1,0:T(8,128)} async-done(((f32[2,64,512]{2,1,0:T(8,128)}), f32[2,1024,512]{2,1,0:T(8,128)}) %all-gather.10.cloned.1.call-update) | async-done | bytes 4194320 | tf_op jit(solution)/shard_map/all_gather | solution.py:54
  414.8 5.0 fusion.4
  419.8 9.1 %all_gather.36 = f32[2,64,1024]{2,1,0:T(8,128)S(1)} all-gather(f32[2,64,512]{2,1,0:T(8,128)S(1)} %fusion.4), channel_id=1, replica_groups=mesh['dp'=16,'grp'=2] {'grp'}, dimensions={2}, use_global_device_ids=true | all-gather | bytes 786432 | tf_op jit(solution)/shard_map/all_gather | solution.py:56
  428.9 4.3 convolution_subtract_fusion.1
  433.3 49.0 %all-gather.12.cloned.1.call-done = f32[2,1024,512]{2,1,0:T(8,128)} async-done(((f32[2,64,512]{2,1,0:T(8,128)}), f32[2,1024,512]{2,1,0:T(8,128)}) %all-gather.12.cloned.1.call-update) | async-done | bytes 4194320 | tf_op jit(solution)/shard_map/all_gather | solution.py:54
  482.4 5.0 fusion.5
  487.4 9.1 %all_gather.38 = f32[2,64,1024]{2,1,0:T(8,128)S(1)} all-gather(f32[2,64,512]{2,1,0:T(8,128)S(1)} %fusion.5), channel_id=1, replica_groups=mesh['dp'=16,'grp'=2] {'grp'}, dimensions={2}, use_global_device_ids=true | all-gather | bytes 786432 | tf_op jit(solution)/shard_map/all_gather | solution.py:56
  496.5 3.6 convolution_subtract_fusion
  500.1 8.5 collective-permute-done
  508.6 8.5 collective-permute-done.1
  517.1 8.5 collective-permute-done.2
  525.6 8.5 collective-permute-done.3
  534.1 8.5 collective-permute-done.4
  542.6 8.5 collective-permute-done.5
  551.1 8.5 collective-permute-done.6
  559.6 8.5 collective-permute-done.7
  568.1 8.5 collective-permute-done.8
  577.3 8.5 collective-permute-done.9
  586.5 8.5 collective-permute-done.10
  595.7 8.5 collective-permute-done.11
  604.9 8.5 collective-permute-done.12
  614.0 8.6 collective-permute-done.13
  622.7 8.8 %collective-permute-done.14 = f32[2,64,512]{2,1,0:T(8,128)} collective-permute-done((f32[2,64,512]{2,1,0:T(8,128)}, f32[2,64,512]{2,1,0:T(8,128)}, u32[]{:S(2)}, u32[]{:S(2)}) %collective-permute-start.14) | collective-permute-done | bytes 262176 | tf_op jit(solution)/shard_map/ppermute | solution.py:61
  633.4 1.0 constant_dynamic-update-slice_fusion.29
  635.3 1.0 constant_dynamic-update-slice_fusion.27
  640.9 2.4 constant_dynamic-slice_fusion
  643.4 101.3 %all-gather.14.cloned.1.call-done = f32[2,1024,1024]{2,1,0:T(8,128)} async-done(((f32[2,1024,512]{2,1,0:T(8,128)}), f32[2,1024,1024]{2,1,0:T(8,128)}) %all-gather.14.cloned.1.call-update) | async-done | bytes 8388624 | tf_op jit(solution)/shard_map/all_gather | solution.py:65
  744.7 8.6 fusion
  753.3 8.6 fusion.1
  761.9 8.3 convolution_multiply_fusion
  770.3 72.9 %reduce-scatter.9.cloned.1.call-done = f32[64,1024]{1,0:T(8,128)} async-done(((f32[1024,1024]{1,0:T(8,128)}), f32[64,1024]{1,0:T(8,128)}) %reduce-scatter.9.cloned.1.call-update) | async-done | bytes 262160 | tf_op jit(solution)/shard_map/reduce_scatter | solution.py:68
  843.3 13.0 %reduce-scatter.11.cloned.1.call-done = f32[64,512]{1,0:T(8,128)} async-done(((f32[64,1024]{1,0:T(8,128)}), f32[64,512]{1,0:T(8,128)}) %reduce-scatter.11.cloned.1.call-update) | async-done | bytes 131088 | tf_op jit(solution)/shard_map/reduce_scatter | solution.py:77
  (104 shorter events, 12.5 us)
Async XLA Ops:
  6.5 2.9 copy-start
  6.5 110.7 %reduce-scatter.5.cloned.1.call-start = ((), (), s32[]{:S(2)}) async-start(), calls=%async_computation.4 | async-start | bytes 12582912 | tf_op jit(solution)/shard_map/reduce_scatter | solution.py:40
  15.0 178.9 %copy-start.16 = (f32[2]{0:T(128)S(1)}, f32[2]{0:T(128)}, u32[]{:S(2)}) copy-start(f32[2]{0:T(128)} %param.5) | copy-start | bytes 28
  15.0 178.9 %reduce-scatter.7.cloned.1.call-start = ((), (), s32[]{:S(2)}) async-start(), calls=%async_computation.5 | async-start | bytes 4456448 | tf_op jit(solution)/shard_map/reduce_scatter | solution.py:41
  117.3 163.3 %all-gather.6.cloned.1.call-start = ((), (), s32[]{:S(2)}) async-start(), calls=%async_computation.6 | async-start | bytes 4456448 | tf_op jit(solution)/shard_map/all_gather | solution.py:54
  232.7 114.4 %all-gather.8.cloned.1.call-start = ((), (), s32[]{:S(2)}) async-start(), calls=%async_computation.7 | async-start | bytes 4456448 | tf_op jit(solution)/shard_map/all_gather | solution.py:54
  280.6 14.1 %copy-start.4 = (f32[2,1024,512]{2,1,0:T(8,128)S(1)}, f32[2,1024,512]{2,1,0:T(8,128)}, u32[]{:S(2)}) copy-start(f32[2,1024,512]{2,1,0:T(8,128)} %all-gather.6.cloned.1.call-done) | copy-start | bytes 12582916
  298.0 116.8 %all-gather.10.cloned.1.call-start = ((), (), s32[]{:S(2)}) async-start(), calls=%async_computation.8 | async-start | bytes 4456448 | tf_op jit(solution)/shard_map/all_gather | solution.py:54
  347.1 14.3 %copy-start.2 = (f32[2,1024,512]{2,1,0:T(8,128)S(1)}, f32[2,1024,512]{2,1,0:T(8,128)}, u32[]{:S(2)}) copy-start(f32[2,1024,512]{2,1,0:T(8,128)} %all-gather.8.cloned.1.call-done) | copy-start | bytes 12582916
  365.7 116.6 %all-gather.12.cloned.1.call-start = ((), (), s32[]{:S(2)}) async-start(), calls=%async_computation.9 | async-start | bytes 4456448 | tf_op jit(solution)/shard_map/all_gather | solution.py:54
  414.8 14.1 %copy-start.3 = (f32[2,1024,512]{2,1,0:T(8,128)S(1)}, f32[2,1024,512]{2,1,0:T(8,128)}, u32[]{:S(2)}) copy-start(f32[2,1024,512]{2,1,0:T(8,128)} %all-gather.10.cloned.1.call-done) | copy-start | bytes 12582916
  433.3 311.5 %all-gather.14.cloned.1.call-start = ((), (), s32[]{:S(2)}) async-start(), calls=%async_computation.10 | async-start | bytes 12582912 | tf_op jit(solution)/shard_map/all_gather | solution.py:65
  482.4 14.1 %copy-start.1 = (f32[2,1024,512]{2,1,0:T(8,128)S(1)}, f32[2,1024,512]{2,1,0:T(8,128)}, u32[]{:S(2)}) copy-start(f32[2,1024,512]{2,1,0:T(8,128)} %all-gather.12.cloned.1.call-done) | copy-start | bytes 12582916
  500.1 8.5 collective-permute-start
  508.6 8.5 collective-permute-start.1
  517.1 8.5 collective-permute-start.2
  525.6 8.5 collective-permute-start.3
  534.1 8.5 collective-permute-start.4
  542.6 8.5 collective-permute-start.5
  551.1 8.5 collective-permute-start.6
  559.6 8.5 collective-permute-start.7
  568.1 8.5 collective-permute-start.8
  576.6 0.7 copy-start.6
  577.3 8.5 collective-permute-start.9
  585.8 0.7 copy-start.8
  586.5 8.5 collective-permute-start.10
  594.9 0.7 copy-start.10
  595.7 8.5 collective-permute-start.11
  604.1 0.7 copy-start.12
  604.8 8.5 collective-permute-start.12
  613.3 0.7 copy-start.14
  614.0 8.6 collective-permute-start.13
  622.6 8.8 %collective-permute-start.14 = (f32[2,64,512]{2,1,0:T(8,128)}, f32[2,64,512]{2,1,0:T(8,128)}, u32[]{:S(2)}, u32[]{:S(2)}) collective-permute-start(f32[2,64,512]{2,1,0:T(8,128)} %collective-permute-done.13), channel_id=1, source_target_pairs={{0,2},{2,4},{4,6},{6,8},{8,10},{10,12},{12,14},{14,16},{16,18},{18... | collective-permute-start | bytes 786440 | tf_op jit(solution)/shard_map/ppermute | solution.py:61
  622.6 17.8 %copy-start.15 = (f32[2,64,512]{2,1,0:T(8,128)S(1)}, f32[2,64,512]{2,1,0:T(8,128)}, u32[]{:S(2)}) copy-start(f32[2,64,512]{2,1,0:T(8,128)} %copy-done.14) | copy-start | bytes 786436
  622.6 17.8 %copy-start.13 = (f32[2,64,512]{2,1,0:T(8,128)S(1)}, f32[2,64,512]{2,1,0:T(8,128)}, u32[]{:S(2)}) copy-start(f32[2,64,512]{2,1,0:T(8,128)} %copy-done.12) | copy-start | bytes 786436
  622.6 17.9 %copy-start.11 = (f32[2,64,512]{2,1,0:T(8,128)S(1)}, f32[2,64,512]{2,1,0:T(8,128)}, u32[]{:S(2)}) copy-start(f32[2,64,512]{2,1,0:T(8,128)} %copy-done.10) | copy-start | bytes 786436
  622.6 17.9 %copy-start.9 = (f32[2,64,512]{2,1,0:T(8,128)S(1)}, f32[2,64,512]{2,1,0:T(8,128)}, u32[]{:S(2)}) copy-start(f32[2,64,512]{2,1,0:T(8,128)} %copy-done.8) | copy-start | bytes 786436
  622.7 17.9 %copy-start.7 = (f32[2,64,512]{2,1,0:T(8,128)S(1)}, f32[2,64,512]{2,1,0:T(8,128)}, u32[]{:S(2)}) copy-start(f32[2,64,512]{2,1,0:T(8,128)} %copy-done.6) | copy-start | bytes 786436
  640.9 112.4 %copy-start.5 = (bf16[512,1024]{1,0:T(8,128)(2,1)S(1)}, bf16[512,1024]{1,0:T(8,128)(2,1)}, u32[]{:S(2)}) copy-start(bf16[512,1024]{1,0:T(8,128)(2,1)} %param.3) | copy-start | bytes 3145732
  643.4 199.9 %reduce-scatter.9.cloned.1.call-start = ((), (), s32[]{:S(2)}) async-start(), calls=%async_computation.11 | async-start | bytes 4456448 | tf_op jit(solution)/shard_map/reduce_scatter | solution.py:68
  770.3 86.0 %reduce-scatter.11.cloned.1.call-start = ((), (), s32[]{:S(2)}) async-start(), calls=%async_computation.12 | async-start | bytes 393216 | tf_op jit(solution)/shard_map/reduce_scatter | solution.py:77
Sparse Core Ops, SparseCore 0:
  15.2 102.0 reduce-scatter.4
  121.1 72.7 reduce-scatter.6
  232.9 47.6 all-gather.5
  298.2 48.9 all-gather.7
  365.9 48.9 all-gather.9
  433.4 48.9 all-gather.11
  643.5 101.2 all-gather.13
  770.4 72.7 reduce-scatter.8
  845.5 10.7 reduce-scatter.10
